TPU v7x, 256 devices: a whole 4x4x8 slice. The times are simulated.
256 devices in a mesh: section: 8 (over z), expert: 2 (over core), tensor: 16 (over y, x).
Axes of the slice: x: 4, y: 4, z: 8, core: 2. Of those that a mesh axis runs over, the one named last changes fastest.
Arguments:
- tokens: bfloat16 [8192, 6144], P(('section', 'expert'), 'tensor'), may hold values from -6 to 6
- norm_gain: float32 [4, 6144], P(None, 'tensor'), may hold values from 0.5 to 1.5
- router: float32 [4, 6144, 8], P(None, 'tensor'), may hold values from -0.078125 to 0.078125
- w_gate: bfloat16 [8, 2, 6144, 4096], P('section', 'expert', None, 'tensor'), may hold values from -0.078125 to 0.078125
- w_up: bfloat16 [8, 2, 6144, 4096], P('section', 'expert', None, 'tensor'), may hold values from -0.078125 to 0.078125
- w_down: bfloat16 [8, 2, 4096, 6144], P('section', 'expert', 'tensor'), may hold values from -0.0625 to 0.0625
- expert_ids: int32 [2, 8192, 2], P(None, ('section', 'expert')), may hold values from 0 to 7, all different within a row
- lengths: int32 [8, 8], P(None, 'expert'), may hold values from 32 to 128
Outputs:
- encoded: bfloat16 [8192, 6144], P(('section', 'expert'), 'tensor')
All inputs are finite; a program needn't handle non-finite values.
Results may differ from a plain program's by a relative error of at most 0.006.
Values may be sent and summed in bfloat16 or wider, within the bound.
A program may use at most 64 MiB of HBM per device.

v0:
```python
import jax
import jax.numpy as jnp
from jax import lax
from jax.sharding import PartitionSpec as P

D = 6144
E = 8
EXP_WIN = 2
SEQ_LEN = 128
STEPS = 2
CAP = 64
norm_eps = 1e-05


def swapped(x, axis, bit):
    return lax.ppermute(x, axis, [(i, i ^ 1 << bit) for i in range(lax.axis_size(axis))])


def from_behind(x, axis, by):
    peers = lax.axis_size(axis)
    return lax.ppermute(x, axis, [(i, (i + by) % peers) for i in range(peers)])


def route_tables(choice_ids, seq_lens, gate_logits):
    token_count = choice_ids.shape[0]
    expert_range = jnp.arange(E, dtype=jnp.int32)
    match_ids = choice_ids[:, :, None] == expert_range[None, None, :]
    one_hot = match_ids.astype(jnp.float32)
    picked = jnp.sum(gate_logits[:, None, :] * one_hot, axis=2)
    first_weight = jax.nn.sigmoid(picked[:, 0] - picked[:, 1])
    second_weight = jax.nn.sigmoid(picked[:, 1] - picked[:, 0])
    dense_gates = (
        first_weight[:, None] * one_hot[:, 0, :] + second_weight[:, None] * one_hot[:, 1, :]
    )
    dense_gates = dense_gates[:, :EXP_WIN]
    positions = jnp.arange(token_count, dtype=jnp.int32)
    live_rows = positions % SEQ_LEN < jnp.repeat(seq_lens, SEQ_LEN, total_repeat_length=token_count)
    named = jnp.any(match_ids, axis=1)[:, :EXP_WIN] & live_rows[:, None]
    named_int = named.astype(jnp.int32)
    earlier = jnp.cumsum(named_int, axis=0) - named_int
    slot_range = jnp.arange(CAP, dtype=jnp.int32)
    placed = named[None, :, :] & (earlier[None, :, :] == slot_range[:, None, None])
    route_table = jnp.transpose(placed.astype(jnp.float32), (2, 0, 1))
    return (route_table, route_table * jnp.transpose(dense_gates)[:, None, :])


def moe_layer(
    layer_rows, gain_row, router_matrix, gate_w, up_w, down_w, choice_ids, seq_lens, expert_count
):
    as_float = layer_rows.astype(jnp.float32)
    scaled = as_float * gain_row[None, :]
    part_logits = jnp.dot(scaled, router_matrix, precision=lax.Precision.HIGHEST)
    square_sum, logit_sum = lax.psum((jnp.sum(as_float * as_float, axis=1), part_logits), "tensor")
    inv_rms = lax.rsqrt(square_sum / D + norm_eps)
    normed = (scaled * inv_rms[:, None]).astype(jnp.bfloat16)
    gate_logits = inv_rms[:, None] * logit_sum
    route_table, weighted = route_tables(choice_ids, seq_lens, gate_logits)
    fsplit_count = expert_count // EXP_WIN
    table_narrow = route_table.astype(jnp.bfloat16)
    feature_count = normed.shape[1]
    picked_rows = jnp.einsum(
        "ecr,rd->ecd", table_narrow, normed, preferred_element_type=jnp.float32
    ).astype(jnp.bfloat16)
    widened = jnp.broadcast_to(picked_rows[:, None], (EXP_WIN, fsplit_count, CAP, feature_count))
    arrived = lax.all_to_all(
        widened.reshape(expert_count, CAP, feature_count),
        "expert",
        split_axis=0,
        concat_axis=1,
        tiled=True,
    )
    partner = swapped(arrived, "section", 0)
    held_rows = jnp.concatenate([arrived, partner], axis=1)
    feature_piece = lax.all_gather(held_rows, "tensor", axis=2, tiled=True)
    col_count = feature_piece.shape[2]
    gate_part = lax.slice_in_dim(gate_w, 0, col_count, axis=1)
    up_part = lax.slice_in_dim(up_w, 0, col_count, axis=1)
    gate_more = jnp.einsum(
        "snd,sdf->snf", feature_piece, gate_part, preferred_element_type=jnp.float32
    )
    up_more = jnp.einsum("snd,sdf->snf", feature_piece, up_part, preferred_element_type=jnp.float32)
    hidden = (jax.nn.silu(gate_more) * up_more).astype(jnp.bfloat16)
    partial_out = jnp.einsum("snf,sfd->snd", hidden, down_w, preferred_element_type=jnp.float32)
    summed = lax.psum_scatter(
        partial_out.astype(jnp.bfloat16), "tensor", scatter_dimension=2, tiled=True
    )
    own_count = summed.shape[1] // 2
    own_part = summed[:, :own_count]
    other_part = summed[:, own_count:]
    from_partner = swapped(other_part, "section", 0)
    slab_out = (own_part.astype(jnp.float32) + from_partner.astype(jnp.float32)).astype(
        jnp.bfloat16
    )
    returned = lax.all_to_all(slab_out, "expert", split_axis=1, concat_axis=0, tiled=True)
    half_width = returned.shape[2]
    per_expert = jnp.sum(
        returned.reshape(EXP_WIN, fsplit_count, CAP, half_width).astype(jnp.float32), axis=1
    )
    mixture = jnp.einsum("ecr,ecd->rd", weighted, per_expert, precision=lax.Precision.HIGHEST)
    return (as_float + mixture).astype(jnp.bfloat16)


def on_device(tokens, norm_gain, router, w_gate, w_up, w_down, expert_ids, lengths):
    section_count = lax.axis_size("section")
    section_place = lax.axis_index("section")
    expert_count = lax.axis_size("expert")
    layer_place = section_place // 2
    gain_row = lax.dynamic_index_in_dim(norm_gain, layer_place, 0, keepdims=False)
    router_matrix = lax.dynamic_index_in_dim(router, layer_place, 0, keepdims=False)
    current = tokens
    for step_index in range(STEPS):
        micro_batch = (section_place - 2 * step_index) % section_count
        seq_lens = lax.dynamic_index_in_dim(lengths, micro_batch, 0, keepdims=False)
        current = moe_layer(
            current,
            gain_row,
            router_matrix,
            w_gate[0],
            w_up[0],
            w_down[0],
            expert_ids[step_index],
            seq_lens,
            expert_count,
        )
        if step_index + 1 < STEPS:
            current = from_behind(current, "section", 2)
    return current


def solution(mesh):
    in_specs = (
        P(("section", "expert"), "tensor"),
        P(None, "tensor"),
        P(None, "tensor", None),
        P("section", "expert", None, "tensor"),
        P("section", "expert", None, "tensor"),
        P("section", "expert", "tensor", None),
        P(None, ("section", "expert"), None),
        P(None, "expert"),
    )
    out_specs = P(("section", "expert"), "tensor")
    return jax.shard_map(
        on_device, mesh=mesh, in_specs=in_specs, out_specs=out_specs, check_vma=False
    )
```

profile of v0, /device:TPU:1, one launch (start us, length us, event | category | flops | bytes accessed | tf_op | source)
XLA Modules:
  0.0 600.9 jit_solution(5741067348918299058)
XLA Ops:
  9.3 1.8 fusion.21
  11.1 61.2 %all-reduce.1 = (f32[512]{0:T(512)S(1)}, f32[512,8]{0,1:T(8,128)}) all-reduce(f32[512]{0:T(512)S(1)} %fusion.26, f32[512,8]{0,1:T(8,128)S(1)} %fusion.21), channel_id=1, replica_groups=mesh['section'=8,'expert'=2,'tensor'=16] {'tensor'}, use_global_device_ids=true, to_apply=%region_4.6 | all-reduce | flops 4608 | bytes 36864 | tf_op jit(solution)/shard_map/psum | solution.py:53
  74.6 2.5 select_compare_fusion.1
  80.2 18.3 %all_to_all.42 = bf16[2,64,384]{2,1,0:T(8,128)(2,1)S(1)} all-to-all(bf16[2,64,384]{2,1,0:T(8,128)(2,1)S(1)} %convolution_convert_fusion.3), channel_id=1, replica_groups=mesh['section'=8,'expert'=2,'tensor'=16] {'expert'}, dimensions={0} | all-to-all | bytes 196608 | tf_op jit(solution)/shard_map/all_to_all | solution.py:65
  100.2 2.7 collective-permute-done
  103.7 53.6 %all-gather.3.cloned.1.call-done = bf16[1,256,6144]{2,1,0:T(8,128)(2,1)} async-done(((bf16[1,256,384]{2,1,0:T(8,128)(2,1)}), bf16[1,256,6144]{2,1,0:T(8,128)(2,1)}) %all-gather.3.cloned.1.call-update) | async-done | bytes 3145744 | tf_op jit(solution)/shard_map/all_gather | solution.py:74
  157.3 3.8 fusion.9
  161.1 8.0 %fusion = bf16[1,256,6144]{2,1,0:T(8,128)(2,1)} fusion(bf16[1,1,256,6144]{3,2,1,0:T(8,128)(2,1)S(1)} %copy-done, f32[256,256]{1,0:T(8,128)S(1)} %fusion.9, bf16[1,1,6144,256]{3,2,1,0:T(8,128)(2,1)} %param.17, bf16[1,256,6144]{2,1,0:T(8,128)(2,1)} %all-gather.3.cloned.1.call-done), kind=kOutput, calls=%fused_computation.2 | convolution fusion | flops 1612578816 | bytes 12845056 | tf_op jit(solution)/shard_map/snf,sfd->snd/dot_general | solution.py:83
  169.1 13.9 %copy.13 = bf16[1,256,6144]{1,0,2:T(2,128)(2,1)} copy(bf16[1,256,6144]{2,1,0:T(8,128)(2,1)} %fusion) | data formatting | bytes 6291456
  183.1 5.0 copy.34
  188.2 2.6 select_compare_fusion
  194.1 75.0 %reduce-scatter.7.cloned.1.call-done = bf16[384,256]{1,0:T(8,128)(2,1)} async-done(((bf16[6144,256]{1,0:T(8,128)(2,1)}), bf16[384,256]{1,0:T(8,128)(2,1)}) %reduce-scatter.7.cloned.1.call-update) | async-done | bytes 196624
  271.4 1.7 copy.22
  279.4 2.7 reduce.13
  283.6 8.5 %all_to_all.43 = bf16[2,2,12288]{2,1,0:T(2,128)(2,1)} all-to-all(bf16[2,2,12288]{2,1,0:T(2,128)(2,1)} %reshape.217), channel_id=1, replica_groups=mesh['section'=8,'expert'=2,'tensor'=16] {'expert'}, dimensions={0} | all-to-all | bytes 196608 | tf_op jit(solution)/shard_map/all_to_all | solution.py:94
  296.0 2.3 collective-permute-start.2
  299.7 14.5 %collective-permute-done.2 = bf16[512,384]{1,0:T(8,128)(2,1)S(1)} collective-permute-done((bf16[512,384]{1,0:T(8,128)(2,1)S(1)}, bf16[512,384]{1,0:T(8,128)(2,1)S(1)}, u32[]{:S(2)}, u32[]{:S(2)}) %collective-permute-start.2) | collective-permute-done | bytes 393248 | tf_op jit(solution)/shard_map/ppermute | solution.py:21
  316.4 58.0 %all-reduce = (f32[512]{0:T(512)}, f32[512,8]{0,1:T(8,128)}) all-reduce(f32[512]{0:T(512)} %fusion.27, f32[512,8]{0,1:T(8,128)S(1)} %fusion.23), channel_id=1, replica_groups=mesh['section'=8,'expert'=2,'tensor'=16] {'tensor'}, use_global_device_ids=true, to_apply=%region_12.14 | all-reduce | flops 4608 | bytes 36864 | tf_op jit(solution)/shard_map/psum | solution.py:53
  376.1 18.4 %all_to_all.44 = bf16[2,64,384]{2,1,0:T(8,128)(2,1)S(1)} all-to-all(bf16[2,64,384]{2,1,0:T(8,128)(2,1)S(1)} %convolution_convert_fusion.2), channel_id=1, replica_groups=mesh['section'=8,'expert'=2,'tensor'=16] {'expert'}, dimensions={0} | all-to-all | bytes 196608 | tf_op jit(solution)/shard_map/all_to_all | solution.py:65
  394.6 4.4 collective-permute-start.3
  398.9 2.8 collective-permute-done.3
  402.5 52.4 %all-gather.5.cloned.1.call-done = bf16[1,256,6144]{2,1,0:T(8,128)(2,1)} async-done(((bf16[1,256,384]{2,1,0:T(8,128)(2,1)}), bf16[1,256,6144]{2,1,0:T(8,128)(2,1)}) %all-gather.5.cloned.1.call-update) | async-done | bytes 3145744 | tf_op jit(solution)/shard_map/all_gather | solution.py:74
  454.9 4.5 fusion.2
  459.4 8.0 %fusion.1 = bf16[1,256,6144]{2,1,0:T(8,128)(2,1)} fusion(bf16[1,1,256,6144]{3,2,1,0:T(8,128)(2,1)S(1)} %copy-done, f32[256,256]{1,0:T(8,128)} %fusion.2, bf16[1,256,6144]{2,1,0:T(8,128)(2,1)} %all-gather.5.cloned.1.call-done, bf16[1,1,6144,256]{3,2,1,0:T(8,128)(2,1)} %param.17), kind=kOutput, calls=%fused_computation.3 | convolution fusion | flops 1612578816 | bytes 12845056 | tf_op jit(solution)/shard_map/snf,sfd->snd/dot_general | solution.py:83
  467.4 13.9 %copy.15 = bf16[1,256,6144]{1,0,2:T(2,128)(2,1)} copy(bf16[1,256,6144]{2,1,0:T(8,128)(2,1)} %fusion.1) | data formatting | bytes 6291456
  481.4 5.0 copy.33
  488.5 78.9 %reduce-scatter.9.cloned.1.call-done = bf16[384,256]{1,0:T(8,128)(2,1)} async-done(((bf16[6144,256]{1,0:T(8,128)(2,1)}), bf16[384,256]{1,0:T(8,128)(2,1)}) %reduce-scatter.9.cloned.1.call-update) | async-done | bytes 196624
  569.7 1.7 copy.24
  573.3 1.7 copy.23
  576.9 2.7 reduce.14
  581.2 8.7 %all_to_all.45 = bf16[2,2,12288]{2,1,0:T(2,128)(2,1)} all-to-all(bf16[2,2,12288]{2,1,0:T(2,128)(2,1)} %reshape.219), channel_id=1, replica_groups=mesh['section'=8,'expert'=2,'tensor'=16] {'expert'}, dimensions={0} | all-to-all | bytes 196608 | tf_op jit(solution)/shard_map/all_to_all | solution.py:94
  592.4 2.0 fusion.18
  (90 shorter events, 46.3 us)
Async XLA Ops:
  6.5 154.6 %copy-start = (bf16[1,1,256,6144]{3,2,1,0:T(8,128)(2,1)S(1)}, bf16[1,1,256,6144]{3,2,1,0:T(8,128)(2,1)}, u32[]{:S(2)}) copy-start(bf16[1,1,256,6144]{3,2,1,0:T(8,128)(2,1)} %param.19) | copy-start | bytes 9437188
  6.5 150.7 %all-gather.3.cloned.1.call-start = ((), (), s32[]{:S(2)}) async-start(), calls=%async_computation.6 | async-start | bytes 3342336 | tf_op jit(solution)/shard_map/all_gather | solution.py:74
  8.5 95.1 %copy-start.2 = (s32[512,2]{0,1:T(2,128)}, s32[512,2]{0,1:T(2,128)S(1)}, u32[]{:S(2)}) copy-start(s32[512,2]{0,1:T(2,128)S(1)} %get-tuple-element.40) | copy-start | bytes 12292
  9.3 94.4 %copy-start.4 = (f32[384]{0:T(512)}, f32[384]{0:T(512)S(1)}, u32[]{:S(2)}) copy-start(f32[384]{0:T(512)S(1)} %dynamic-slice_reduce_fusion.2) | copy-start | bytes 4612
  72.3 31.3 %copy-start.5 = (f32[512]{0:T(512)}, f32[512]{0:T(512)S(1)}, u32[]{:S(2)}) copy-start(f32[512]{0:T(512)S(1)} %add_rsqrt_fusion.1) | copy-start | bytes 6148
  77.2 26.5 %copy-start.10 = (pred[2,512]{1,0:T(4,128)(4,1)}, pred[2,512]{1,0:T(4,128)(4,1)S(1)}, u32[]{:S(2)}) copy-start(pred[2,512]{1,0:T(4,128)(4,1)S(1)} %get-tuple-element.44) | copy-start | bytes 3076
  78.3 0.6 copy-start.8
  98.5 4.3 collective-permute-start
  103.6 165.5 %reduce-scatter.7.cloned.1.call-start = ((), (), s32[]{:S(2)}) async-start(), calls=%async_computation.8 | async-start | bytes 3342336
  188.1 106.7 %copy-start.1 = (bf16[512,384]{1,0:T(8,128)(2,1)S(1)}, bf16[512,384]{1,0:T(8,128)(2,1)}, u32[]{:S(2)}) copy-start(bf16[512,384]{1,0:T(8,128)(2,1)} %param.14) | copy-start | bytes 1179652
  188.1 266.8 %all-gather.5.cloned.1.call-start = ((), (), s32[]{:S(2)}) async-start(), calls=%async_computation.7 | async-start | bytes 3342336 | tf_op jit(solution)/shard_map/all_gather | solution.py:74
  190.8 0.6 copy-start.6
  192.0 107.1 %copy-start.7 = (pred[512]{0:T(512)(128)(4,1)S(1)}, pred[512]{0:T(512)(128)(4,1)}, u32[]{:S(2)}) copy-start(pred[512]{0:T(512)(128)(4,1)} %copy-done.6) | copy-start | bytes 1540
  273.1 3.9 collective-permute-start.1
  296.0 18.2 %collective-permute-start.2 = (bf16[512,384]{1,0:T(8,128)(2,1)S(1)}, bf16[512,384]{1,0:T(8,128)(2,1)S(1)}, u32[]{:S(2)}, u32[]{:S(2)}) collective-permute-start(bf16[512,384]{1,0:T(8,128)(2,1)S(1)} %fusion.19), channel_id=1, source_target_pairs={{0,64},{32,96},{64,128},{96,160},{128,192},{160,224},{192,0},{224,... | collective-permute-start | bytes 1179656 | tf_op jit(solution)/shard_map/ppermute | solution.py:21
  394.6 7.2 %collective-permute-start.3 = (bf16[1,128,384]{2,1,0:T(8,128)(2,1)S(1)}, bf16[1,128,384]{2,1,0:T(8,128)(2,1)S(1)}, u32[]{:S(2)}, u32[]{:S(2)}) collective-permute-start(bf16[1,128,384]{2,1,0:T(8,128)(2,1)S(1)} %bitcast.192), channel_id=1, source_target_pairs={{0,32},{32,0},{64,96},{96,64},{128,160},{160,128},{192,224},{224,1... | collective-permute-start | bytes 294920 | tf_op jit(solution)/shard_map/ppermute | solution.py:16
  402.5 164.9 %reduce-scatter.9.cloned.1.call-start = ((), (), s32[]{:S(2)}) async-start(), calls=%async_computation.9 | async-start | bytes 3342336
  486.4 2.1 copy-start.3
  486.4 106.1 %copy-start.9 = (s32[2,512]{1,0:T(2,128)S(1)}, s32[2,512]{1,0:T(2,128)}, u32[]{:S(2)}) copy-start(s32[2,512]{1,0:T(2,128)} %fusion.83) | copy-start | bytes 12292
  571.3 3.8 collective-permute-start.4
Sparse Core Ops, SparseCore 0:
  103.7 53.5 all-gather.2
  188.2 80.8 reduce-scatter.6
  402.6 52.2 all-gather.4
  486.5 80.8 reduce-scatter.8
where the time goes:
time: 603 us; the launch traced here: 601 us
  waiting for transfers between devices  280 us (46%)
  blocking collectives  173 us (29%)
  local copies, waits for them, and re-layouts  65.9 us (11%)
  matrix products  33.2 us (6%)
  other arithmetic  24.3 us (4%)
  between operations  13.3 us (2%)
  starting transfers between devices  11 us (2%)
    unnamed x6, waiting for transfers between devices  154 us
    psum x2, blocking collectives, moe_layer(): lax.psum((jnp.sum(as_float * as_float, axis=1), part_logits), 'tensor')  119 us
    all_gather x2, waiting for transfers between devices, moe_layer(): feature_piece = lax.all_gather(held_rows, 'tensor', axis=2, tiled=True)  106 us
    unnamed x39, local copies, waits for them, and re-layouts  56.4 us
    all_to_all x2, blocking collectives, moe_layer(): lax.all_to_all(widened.reshape(expert_count, CAP, feature_count), 'expert...  36.8 us
    all_to_all x2, blocking collectives, moe_layer(): lax.all_to_all(slab_out, 'expert', split_axis=1, concat_axis=0, tiled=True)  17.2 us
    dot_general x2, matrix products, moe_layer(): jnp.einsum('snf,sfd->snd', hidden, down_w, preferred_element_type=jnp.flo...  16 us
    ppermute x1, waiting for transfers between devices, from_behind(): return lax.ppermute(x, axis, [(i, (i + by) % peers) for i in range(peers)])  14.5 us
  transfers between devices with their start and end apart: 9, of which 8 were waited for; matrix products, arithmetic and copies ran while one was open for 2% of the time, Pallas kernels for 0%

commit v1 on v0

--- a/solution.py
+++ b/solution.py
@@ -71,7 +71,15 @@
     )
     partner = swapped(arrived, "section", 0)
     held_rows = jnp.concatenate([arrived, partner], axis=1)
-    feature_piece = lax.all_gather(held_rows, "tensor", axis=2, tiled=True)
+    feature_piece = jnp.concatenate(
+        lax.all_to_all(
+            jnp.stack([held_rows for _ in range(lax.axis_size("tensor"))]),
+            axis_name="tensor",
+            split_axis=0,
+            concat_axis=0,
+        ),
+        2,
+    )
     col_count = feature_piece.shape[2]
     gate_part = lax.slice_in_dim(gate_w, 0, col_count, axis=1)
     up_part = lax.slice_in_dim(up_w, 0, col_count, axis=1)

time: 603 us -> 579 us (0.960)
  waiting for transfers between devices: 280 us -> 171 us
  blocking collectives: 173 us -> 256 us
  local copies, waits for them, and re-layouts: 65.9 us -> 72.7 us
    all_gather x2 -> x0, waiting for transfers between devices: 106 us -> none  [moe_layer(): feature_piece = lax.all_gather(held_rows, 'tensor', axis=2, tiled=True)]
    all_to_all x0 -> x2, blocking collectives: none -> 82.9 us  [moe_layer(): lax.all_to_all(jnp.stack([held_rows for _ in range(lax.axis_size('tensor'...]
    unnamed x39 -> x47, local copies, waits for them, and re-layouts: 56.4 us -> 59.8 us
    unnamed x6 -> x4, waiting for transfers between devices: 154 us -> 151 us
  transfers between devices with their start and end apart: 9 -> 7, of which waited for: 8 -> 6; matrix products, arithmetic and copies ran while one was open for 2% -> 2% of each run, Pallas kernels for 0% -> 0%
where the time goes in v1:
time: 579 us; the launch traced here: 576 us
  blocking collectives  256 us (44%)
  waiting for transfers between devices  171 us (30%)
  local copies, waits for them, and re-layouts  72.7 us (13%)
  matrix products  27.6 us (5%)
  other arithmetic  23.7 us (4%)
  between operations  13.6 us (2%)
  starting transfers between devices  11 us (2%)
    unnamed x4, waiting for transfers between devices  151 us
    psum x2, blocking collectives, moe_layer(): lax.psum((jnp.sum(as_float * as_float, axis=1), part_logits), 'tensor')  119 us
    all_to_all x2, blocking collectives, moe_layer(): lax.all_to_all(jnp.stack([held_rows for _ in range(lax.axis_size('tensor'...  82.9 us
    unnamed x47, local copies, waits for them, and re-layouts  59.8 us
    all_to_all x2, blocking collectives, moe_layer(): lax.all_to_all(widened.reshape(expert_count, CAP, feature_count), 'expert...  36.8 us
    all_to_all x2, blocking collectives, moe_layer(): lax.all_to_all(slab_out, 'expert', split_axis=1, concat_axis=0, tiled=True)  17.2 us
    dot_general x2, matrix products, moe_layer(): jnp.einsum('snf,sfd->snd', hidden, down_w, preferred_element_type=jnp.flo...  16.1 us
    ppermute x1, waiting for transfers between devices, from_behind(): return lax.ppermute(x, axis, [(i, (i + by) % peers) for i in range(peers)])  14.5 us
  transfers between devices with their start and end apart: 7, of which 6 were waited for; matrix products, arithmetic and copies ran while one was open for 2% of the time, Pallas kernels for 0%

profile of v1, /device:TPU:1, one launch (start us, length us, event | category | flops | bytes accessed | tf_op | source)
XLA Modules:
  0.0 576.2 jit_solution(17658424512175005526)
XLA Ops:
  9.3 1.8 fusion.29
  11.1 61.2 %all-reduce.1 = (f32[512]{0:T(512)S(1)}, f32[512,8]{0,1:T(8,128)}) all-reduce(f32[512]{0:T(512)S(1)} %fusion.34, f32[512,8]{0,1:T(8,128)S(1)} %fusion.29), channel_id=1, replica_groups=mesh['section'=8,'expert'=2,'tensor'=16] {'tensor'}, use_global_device_ids=true, to_apply=%region_4.6 | all-reduce | flops 4608 | bytes 36864 | tf_op jit(solution)/shard_map/psum | solution.py:53
  74.6 2.6 select_compare_fusion.1
  80.3 18.3 %all_to_all.52 = bf16[2,64,384]{2,1,0:T(8,128)(2,1)S(1)} all-to-all(bf16[2,64,384]{2,1,0:T(8,128)(2,1)S(1)} %convolution_convert_fusion.3), channel_id=1, replica_groups=mesh['section'=8,'expert'=2,'tensor'=16] {'expert'}, dimensions={0} | all-to-all | bytes 196608 | tf_op jit(solution)/shard_map/all_to_all | solution.py:65
  100.2 2.7 collective-permute-done
  103.4 41.5 %all_to_all.53 = bf16[16,1,256,384]{2,3,1,0:T(8,128)(2,1)S(1)} all-to-all(bf16[16,1,256,384]{2,3,1,0:T(8,128)(2,1)S(1)} %stack.4), channel_id=1, replica_groups=mesh['section'=8,'expert'=2,'tensor'=16] {'tensor'}, dimensions={0} | all-to-all | bytes 6291456 | tf_op jit(solution)/shard_map/all_to_all | solution.py:75
  147.6 8.0 %fusion = bf16[1,256,6144]{2,1,0:T(8,128)(2,1)} fusion(bf16[1,1,256,6144]{3,2,1,0:T(8,128)(2,1)S(1)} %copy-done, bf16[256,6144]{0,1:T(8,128)(2,1)} %bitcast.191, bf16[1,1,6144,256]{3,2,1,0:T(8,128)(2,1)} %param.18, f32[256,256]{1,0:T(8,128)S(1)} %fusion.10), kind=kOutput, calls=%fused_computation.2 | convolution fusion | flops 1612578816 | bytes 12845056 | tf_op jit(solution)/shard_map/snf,sfd->snd/dot_general | solution.py:91
  155.7 13.9 %copy.23 = bf16[1,256,6144]{1,0,2:T(2,128)(2,1)} copy(bf16[1,256,6144]{2,1,0:T(8,128)(2,1)} %fusion) | data formatting | bytes 6291456
  169.6 5.0 copy.44
  174.7 2.5 select_compare_fusion
  180.5 74.4 %reduce-scatter.7.cloned.1.call-done = bf16[384,256]{1,0:T(8,128)(2,1)} async-done(((bf16[6144,256]{1,0:T(8,128)(2,1)}), bf16[384,256]{1,0:T(8,128)(2,1)}) %reduce-scatter.7.cloned.1.call-update) | async-done | bytes 196624
  257.2 1.7 copy.32
  261.1 1.7 copy.31
  265.2 2.8 reduce.13
  269.5 8.5 %all_to_all.54 = bf16[2,2,12288]{2,1,0:T(2,128)(2,1)} all-to-all(bf16[2,2,12288]{2,1,0:T(2,128)(2,1)} %reshape.237), channel_id=1, replica_groups=mesh['section'=8,'expert'=2,'tensor'=16] {'expert'}, dimensions={0} | all-to-all | bytes 196608 | tf_op jit(solution)/shard_map/all_to_all | solution.py:102
  281.9 2.5 collective-permute-start.2
  285.7 14.5 %collective-permute-done.2 = bf16[512,384]{1,0:T(8,128)(2,1)S(1)} collective-permute-done((bf16[512,384]{1,0:T(8,128)(2,1)S(1)}, bf16[512,384]{1,0:T(8,128)(2,1)S(1)}, u32[]{:S(2)}, u32[]{:S(2)}) %collective-permute-start.2) | collective-permute-done | bytes 393248 | tf_op jit(solution)/shard_map/ppermute | solution.py:21
  302.5 58.1 %all-reduce = (f32[512]{0:T(512)}, f32[512,8]{0,1:T(8,128)}) all-reduce(f32[512]{0:T(512)} %fusion.35, f32[512,8]{0,1:T(8,128)S(1)} %fusion.31), channel_id=1, replica_groups=mesh['section'=8,'expert'=2,'tensor'=16] {'tensor'}, use_global_device_ids=true, to_apply=%region_12.14 | all-reduce | flops 4608 | bytes 36864 | tf_op jit(solution)/shard_map/psum | solution.py:53
  362.2 18.4 %all_to_all.55 = bf16[2,64,384]{2,1,0:T(8,128)(2,1)S(1)} all-to-all(bf16[2,64,384]{2,1,0:T(8,128)(2,1)S(1)} %convolution_convert_fusion.2), channel_id=1, replica_groups=mesh['section'=8,'expert'=2,'tensor'=16] {'expert'}, dimensions={0} | all-to-all | bytes 196608 | tf_op jit(solution)/shard_map/all_to_all | solution.py:65
  380.7 4.3 collective-permute-start.3
  384.9 2.8 collective-permute-done.3
  388.5 1.7 copy.20
  391.4 41.5 %all_to_all.56 = bf16[16,1,256,384]{2,3,1,0:T(8,128)(2,1)S(1)} all-to-all(bf16[16,1,256,384]{2,3,1,0:T(8,128)(2,1)S(1)} %stack.5), channel_id=1, replica_groups=mesh['section'=8,'expert'=2,'tensor'=16] {'tensor'}, dimensions={0} | all-to-all | bytes 6291456 | tf_op jit(solution)/shard_map/all_to_all | solution.py:75
  434.6 1.7 fusion.8
  436.3 8.0 %fusion.1 = bf16[1,256,6144]{2,1,0:T(8,128)(2,1)} fusion(bf16[1,1,256,6144]{3,2,1,0:T(8,128)(2,1)S(1)} %copy-done, bf16[256,6144]{0,1:T(8,128)(2,1)} %bitcast.193, bf16[1,1,6144,256]{3,2,1,0:T(8,128)(2,1)} %param.18, f32[256,256]{1,0:T(8,128)} %fusion.8), kind=kOutput, calls=%fused_computation.3 | convolution fusion | flops 1612578816 | bytes 12845056 | tf_op jit(solution)/shard_map/snf,sfd->snd/dot_general | solution.py:91
  444.3 13.9 %copy.25 = bf16[1,256,6144]{1,0,2:T(2,128)(2,1)} copy(bf16[1,256,6144]{2,1,0:T(8,128)(2,1)} %fusion.1) | data formatting | bytes 6291456
  458.3 5.0 copy.43
  465.4 76.9 %reduce-scatter.9.cloned.1.call-done = bf16[384,256]{1,0:T(8,128)(2,1)} async-done(((bf16[6144,256]{1,0:T(8,128)(2,1)}), bf16[384,256]{1,0:T(8,128)(2,1)}) %reduce-scatter.9.cloned.1.call-update) | async-done | bytes 196624
  544.6 1.7 copy.34
  551.8 2.8 reduce.14
  556.2 8.6 %all_to_all.57 = bf16[2,2,12288]{2,1,0:T(2,128)(2,1)} all-to-all(bf16[2,2,12288]{2,1,0:T(2,128)(2,1)} %reshape.239), channel_id=1, replica_groups=mesh['section'=8,'expert'=2,'tensor'=16] {'expert'}, dimensions={0} | all-to-all | bytes 196608 | tf_op jit(solution)/shard_map/all_to_all | solution.py:102
  567.4 2.0 fusion.14
  (98 shorter events, 51.5 us)
Async XLA Ops:
  6.5 141.1 %copy-start = (bf16[1,1,256,6144]{3,2,1,0:T(8,128)(2,1)S(1)}, bf16[1,1,256,6144]{3,2,1,0:T(8,128)(2,1)}, u32[]{:S(2)}) copy-start(bf16[1,1,256,6144]{3,2,1,0:T(8,128)(2,1)} %param.19) | copy-start | bytes 9437188
  6.5 248.4 %reduce-scatter.7.cloned.1.call-start = ((), (), s32[]{:S(2)}) async-start(), calls=%async_computation.8 | async-start | bytes 3342336
  8.5 94.4 %copy-start.4 = (s32[512,2]{0,1:T(2,128)}, s32[512,2]{0,1:T(2,128)S(1)}, u32[]{:S(2)}) copy-start(s32[512,2]{0,1:T(2,128)S(1)} %get-tuple-element.40) | copy-start | bytes 12292
  9.3 93.7 %copy-start.6 = (f32[384]{0:T(512)}, f32[384]{0:T(512)S(1)}, u32[]{:S(2)}) copy-start(f32[384]{0:T(512)S(1)} %dynamic-slice_reduce_fusion.2) | copy-start | bytes 4612
  72.3 30.6 %copy-start.7 = (f32[512]{0:T(512)}, f32[512]{0:T(512)S(1)}, u32[]{:S(2)}) copy-start(f32[512]{0:T(512)S(1)} %add_rsqrt_fusion.1) | copy-start | bytes 6148
  77.2 25.7 %copy-start.12 = (pred[2,512]{1,0:T(4,128)(4,1)}, pred[2,512]{1,0:T(4,128)(4,1)S(1)}, u32[]{:S(2)}) copy-start(pred[2,512]{1,0:T(4,128)(4,1)S(1)} %get-tuple-element.44) | copy-start | bytes 3076
  78.3 0.6 copy-start.10
  98.6 4.4 collective-permute-start
  103.4 43.2 %copy-start.13 = (bf16[1,1,6144,256]{3,2,1,0:T(8,128)(2,1)S(1)}, bf16[1,1,6144,256]{3,2,1,0:T(8,128)(2,1)}, u32[]{:S(2)}) copy-start(bf16[1,1,6144,256]{3,2,1,0:T(8,128)(2,1)} %param.17) | copy-start | bytes 9437188
  144.9 1.7 copy-start.1
  174.6 106.0 %copy-start.3 = (bf16[512,384]{1,0:T(8,128)(2,1)S(1)}, bf16[512,384]{1,0:T(8,128)(2,1)}, u32[]{:S(2)}) copy-start(bf16[512,384]{1,0:T(8,128)(2,1)} %param.14) | copy-start | bytes 1179652
  174.6 367.6 %reduce-scatter.9.cloned.1.call-start = ((), (), s32[]{:S(2)}) async-start(), calls=%async_computation.9 | async-start | bytes 3342336
  177.2 0.6 copy-start.8
  178.4 106.7 %copy-start.9 = (pred[512]{0:T(512)(128)(4,1)S(1)}, pred[512]{0:T(512)(128)(4,1)}, u32[]{:S(2)}) copy-start(pred[512]{0:T(512)(128)(4,1)} %copy-done.8) | copy-start | bytes 1540
  258.9 3.9 collective-permute-start.1
  281.9 18.3 %collective-permute-start.2 = (bf16[512,384]{1,0:T(8,128)(2,1)S(1)}, bf16[512,384]{1,0:T(8,128)(2,1)S(1)}, u32[]{:S(2)}, u32[]{:S(2)}) collective-permute-start(bf16[512,384]{1,0:T(8,128)(2,1)S(1)} %fusion.15), channel_id=1, source_target_pairs={{0,64},{32,96},{64,128},{96,160},{128,192},{160,224},{192,0},{224,... | collective-permute-start | bytes 1179656 | tf_op jit(solution)/shard_map/ppermute | solution.py:21
  380.7 7.1 %collective-permute-start.3 = (bf16[1,128,384]{2,1,0:T(8,128)(2,1)S(1)}, bf16[1,128,384]{2,1,0:T(8,128)(2,1)S(1)}, u32[]{:S(2)}, u32[]{:S(2)}) collective-permute-start(bf16[1,128,384]{2,1,0:T(8,128)(2,1)S(1)} %bitcast.200), channel_id=1, source_target_pairs={{0,32},{32,0},{64,96},{96,64},{128,160},{160,128},{192,224},{224,1... | collective-permute-start | bytes 294920 | tf_op jit(solution)/shard_map/ppermute | solution.py:16
  391.4 43.1 %copy-start.14 = (bf16[1,1,6144,256]{3,2,1,0:T(8,128)(2,1)S(1)}, bf16[1,1,6144,256]{3,2,1,0:T(8,128)(2,1)}, u32[]{:S(2)}) copy-start(bf16[1,1,6144,256]{3,2,1,0:T(8,128)(2,1)} %param.17) | copy-start | bytes 9437188
  432.9 1.7 copy-start.2
  463.3 2.1 copy-start.5
  463.3 104.1 %copy-start.11 = (s32[2,512]{1,0:T(2,128)S(1)}, s32[2,512]{1,0:T(2,128)}, u32[]{:S(2)}) copy-start(s32[2,512]{1,0:T(2,128)} %fusion.89) | copy-start | bytes 12292
  546.2 3.8 collective-permute-start.4
Sparse Core Ops, SparseCore 0:
  174.8 80.1 reduce-scatter.6
  463.4 78.8 reduce-scatter.8
